TPU v7x, 32 devices: a whole 2x2x4 slice. The times are simulated.
32 devices in a mesh: row: 2 (over y), col: 4 (over z), layer: 4 (over x, core).
Axes of the slice: x: 2, y: 2, z: 4, core: 2. Of those that a mesh axis runs over, the one named last changes fastest.
Arguments:
- eigvecs: float32 [16384, 8192], P('row', ('col', 'layer')), may hold values from -6 to 6
- first_vectors: float32 [16384, 128], P(('row', 'layer'), 'col'), may hold values from -0.375 to 0.375
- second_vectors: float32 [16384, 128], P(('row', 'layer'), 'col'), may hold values from -0.375 to 0.375
- first_factors: float32 [8192, 128], P(('row', 'layer'), 'col'), may hold values from -0.5 to 0.5
- second_factors: float32 [8192, 128], P(('row', 'layer'), 'col'), may hold values from -0.5 to 0.5
- panel_vectors: float32 [16384, 256], P(('row', 'layer')), may hold values from -0.125 to 0.125
- panel_factor: float32 [256, 256], replicated, may hold values from -0.375 to 0.375
Outputs:
- transformed: float32 [16384, 8192], P(('row', 'layer'), 'col')
All inputs are finite; a program needn't handle non-finite values.
Results may differ from a plain program's by a relative error of at most 0.000082.
Values sent between devices are 32-bit elements; how exact they have to be, the bound alone decides.
No kernel may reach another device: no remote copies, remote signals or barrier semaphores. Data moves between devices by JAX's collectives and lax.ppermute only.
A program may use at most 128 MiB of HBM per device.

v0:
```python
import jax
import jax.numpy as jnp
from jax import lax
from jax.sharding import PartitionSpec as P


def with_halo(array, sides, width):
    for axis, dim in sides:
        devices, length = (lax.axis_size(axis), array.shape[dim])
        up = [(i, (i + 1) % devices) for i in range(devices - 1)]
        down = [(j, i) for i, j in up]
        last = lax.slice_in_dim(array, length - width, length, axis=dim)
        first = lax.slice_in_dim(array, 0, width, axis=dim)
        before = lax.ppermute(last, axis, up)
        after = lax.ppermute(first, axis, down)
        array = jnp.concatenate([before, array, after], axis=dim)
    return array


def from_behind(value, axis, steps):
    count = lax.axis_size(axis)
    first, last = (max(0, -steps), min(count, count - steps))
    return lax.ppermute(value, axis, [(source, source + steps) for source in range(first, last)])


def apply_windows(data, vectors, factors):
    count = factors.shape[0] // 128
    width = data.shape[1]
    blocks = data.reshape(count, 256, width)
    vec_blocks = vectors.reshape(count, 256, 128)
    tri_blocks = jnp.triu(factors.reshape(count, 128, 128))
    proj = jnp.einsum("kri,krc->kic", vec_blocks, blocks, precision=lax.Precision.HIGHEST)
    scaled = jnp.einsum("kij,kjc->kic", tri_blocks, proj, precision=lax.Precision.HIGHEST)
    update = jnp.einsum("kri,kic->krc", vec_blocks, scaled, precision=lax.Precision.HIGHEST)
    return (blocks - update).reshape(count * 256, width)


def band_sweeps(data, vec_first, vec_second, fac_first, fac_second, extend, following):
    height = data.shape[0]
    width = data.shape[1]
    aligned = apply_windows(data, vec_first, fac_first)
    padded = extend(jnp.concatenate([aligned, vec_second], axis=1))
    next_factor = following(fac_second[:128])
    extended = jnp.concatenate([fac_second, next_factor], axis=0)
    offset = apply_windows(padded[:, :width], padded[:, width:], extended)
    return offset[128 : height + 128]


def band_tile(data, vec_first, vec_second, fac_first, fac_second):

    def extend(joined):
        return with_halo(joined, ((("row", "layer"), 0),), 128)

    def following(factor):
        return from_behind(factor, ("row", "layer"), -1)

    return band_sweeps(data, vec_first, vec_second, fac_first, fac_second, extend, following)


def to_tiles(data):
    return lax.all_to_all(data, "layer", split_axis=0, concat_axis=1, tiled=True)


def panel_tile(data, panel_vectors, upper):
    partial_value = jnp.dot(
        panel_vectors.T, data, precision=lax.Precision.HIGHEST, preferred_element_type=jnp.float32
    )
    projection = lax.psum(partial_value, ("row", "layer"))
    weights = jnp.dot(
        upper, projection, precision=lax.Precision.HIGHEST, preferred_element_type=jnp.float32
    )
    return data - jnp.dot(
        panel_vectors, weights, precision=lax.Precision.HIGHEST, preferred_element_type=jnp.float32
    )


def on_device(
    eigvecs,
    first_vectors,
    second_vectors,
    first_factors,
    second_factors,
    panel_vectors,
    panel_factor,
):
    upper = jnp.triu(panel_factor)
    reflectors = (
        lax.all_gather(first_vectors, "col", axis=1, tiled=True),
        lax.all_gather(second_vectors, "col", axis=1, tiled=True),
        lax.all_gather(first_factors, "col", axis=1, tiled=True),
        lax.all_gather(second_factors, "col", axis=1, tiled=True),
    )
    tiles = to_tiles(eigvecs)
    tiles = band_tile(tiles, reflectors[0], reflectors[1], reflectors[2], reflectors[3])
    return panel_tile(tiles, panel_vectors, upper)


def solution(mesh):
    in_specs = (
        P("row", ("col", "layer")),
        P(("row", "layer"), "col"),
        P(("row", "layer"), "col"),
        P(("row", "layer"), "col"),
        P(("row", "layer"), "col"),
        P(("row", "layer"), None),
        P(),
    )
    out_specs = P(("row", "layer"), "col")
    return jax.shard_map(
        on_device, mesh=mesh, in_specs=in_specs, out_specs=out_specs, check_vma=False
    )
```

profile of v0, /device:TPU:0, one launch (start us, length us, event | category | flops | bytes accessed | tf_op | source)
XLA Modules:
  0.0 561.3 jit_solution(13967101943740955004)
XLA Ops:
  6.5 7.1 %all-to-all-start = ((f32[4,2048,512]{2,1,0:T(8,128)}), f32[4,2048,512]{2,1,0:T(8,128)}, u32[]{:S(2)}, u32[]{:S(2)}) async-start(f32[4,2048,512]{2,1,0:T(8,128)} %bitcast.38), calls=%async_computation | async-start | bytes 33554432 | tf_op jit(solution)/shard_map/all_to_all | solution.py:61
  15.2 20.1 %all_gather.12 = f32[1024,128]{0,1:T(8,128)S(1)} all-gather(f32[1024,32]{0,1:T(8,128)S(1)} %copy-done.6), channel_id=1, replica_groups=mesh['row'=2,'col'=4,'layer'=4] {'col'}, dimensions={1}, use_global_device_ids=true | all-gather | bytes 655360 | tf_op jit(solution)/shard_map/all_gather | solution.py:90
  36.5 13.3 %all-gather.3.cloned.1.call-done = f32[2048,128]{0,1:T(8,128)} async-done(((f32[2048,32]{0,1:T(8,128)}), f32[2048,128]{0,1:T(8,128)}) %all-gather.3.cloned.1.call-update) | async-done | bytes 1048592 | tf_op jit(solution)/shard_map/all_gather | solution.py:88
  49.8 2.6 copy.41
  52.4 26.1 %all-gather.5.cloned.1.call-done = f32[2048,128]{0,1:T(8,128)} async-done(((f32[2048,32]{0,1:T(8,128)}), f32[2048,128]{0,1:T(8,128)}) %all-gather.5.cloned.1.call-update) | async-done | bytes 1048592 | tf_op jit(solution)/shard_map/all_gather | solution.py:89
  78.5 1.5 copy.43
  80.1 117.2 %all-to-all-done = f32[4,2048,512]{2,1,0:T(8,128)} async-done(((f32[4,2048,512]{2,1,0:T(8,128)}), f32[4,2048,512]{2,1,0:T(8,128)}, u32[]{:S(2)}, u32[]{:S(2)}) %all-to-all-start) | async-done | bytes 16777248 | tf_op jit(solution)/shard_map/all_to_all | solution.py:61
  197.3 20.9 %copy.39 = f32[2048,4,512]{2,1,0:T(4,128)} copy(f32[2048,4,512]{2,0,1:T(8,128)} %bitcast.1) | data formatting | bytes 33554432 | tf_op jit(solution)/shard_map/all_to_all | solution.py:61
  218.2 20.5 %reshape.28 = f32[8,256,2048]{2,1,0:T(8,128)} reshape(f32[2048,4,512]{2,1,0:T(4,128)} %copy.39) | data formatting | bytes 33554432 | tf_op jit(solution)/shard_map/reshape | solution.py:29
  238.8 14.5 %fusion.16 = f32[8,128,2048]{2,1,0:T(8,128)S(1)} fusion(f32[8,256,128]{2,1,0:T(8,128)} %bitcast.41, f32[8,256,2048]{2,1,0:T(8,128)} %reshape.28), kind=kOutput, calls=%fused_computation.29 | convolution fusion | flops 6442450944 | bytes 26214400 | tf_op jit(solution)/shard_map/kri,krc->kic/dot_general | solution.py:32
  253.3 9.6 %fusion.2 = f32[8,128,2048]{2,1,0:T(8,128)} fusion(f32[8,128,2048]{2,1,0:T(8,128)S(1)} %fusion.16, f32[8,128,128]{2,1,0:T(8,128)S(1)} %bitcast.44, pred[128,128]{1,0:T(8,128)(4,1)S(1)} %iota_compare_fusion.2), kind=kOutput, calls=%fused_computation.11 | convolution fusion | flops 3221356544 | bytes 17317888 | tf_op jit(solution)/shard_map/kij,kjc->kic/dot_general | solution.py:33
  262.9 22.4 %bitcast_subtract_fusion.1 = f32[8,256,2048]{2,1,0:T(8,128)} fusion(f32[8,256,2048]{2,1,0:T(8,128)} %reshape.28, f32[8,128,2048]{2,1,0:T(8,128)} %fusion.2, f32[8,256,128]{2,1,0:T(8,128)S(1)} %bitcast.42), kind=kOutput, calls=%fused_computation.2 | convolution fusion | flops 6446645248 | bytes 42991616 | tf_op jit(solution)/shard_map/kri,kic->krc/dot_general | solution.py:34
  285.4 3.1 pad_maximum_fusion.3
  288.5 2.3 collective-permute-start
  290.8 1.3 collective-permute-start.1
  292.1 18.3 %all_gather.15 = f32[1024,128]{0,1:T(8,128)} all-gather(f32[1024,32]{0,1:T(8,128)S(1)} %copy-done.7), channel_id=1, replica_groups=mesh['row'=2,'col'=4,'layer'=4] {'col'}, dimensions={1}, use_global_device_ids=true | all-gather | bytes 655360 | tf_op jit(solution)/shard_map/all_gather | solution.py:91
  310.3 2.0 copy.45
  313.2 1.3 collective-permute-start.2
  314.5 1.8 collective-permute-done.2
  316.4 1.9 pad_maximum_fusion.4
  318.3 19.1 %pad_maximum_fusion = f32[2304,2176]{1,0:T(8,128)} fusion(f32[128,2176]{1,0:T(8,128)} %collective-permute-done.1, f32[2048,128]{1,0:T(8,128)S(1)} %copy.43, f32[2048,2048]{1,0:T(8,128)} %bitcast.30, f32[128,2176]{1,0:T(8,128)} %collective-permute-done), kind=kLoop, calls=%fused_computation | loop fusion | flops 15040512 | bytes 40108032 | tf_op jit(solution)/shard_map/concatenate | solution.py:16
  337.4 15.5 %slice.24 = f32[2304,2048]{1,0:T(8,128)} slice(f32[2304,2176]{1,0:T(8,128)} %pad_maximum_fusion), slice={[0:2304], [0:2048]} | slice | bytes 37748736 | tf_op jit(solution)/shard_map/slice | solution.py:45
  353.9 14.0 %fusion.17 = f32[9,128,2048]{2,1,0:T(8,128)S(1)} fusion(f32[9,256,128]{2,1,0:T(8,128)S(1)} %bitcast.39, f32[9,256,2048]{2,1,0:T(8,128)} %bitcast.34), kind=kOutput, calls=%fused_computation.30 | convolution fusion | flops 7247757312 | bytes 29491200 | tf_op jit(solution)/shard_map/kri,krc->kic/dot_general | solution.py:32
  367.9 11.8 %fusion = f32[9,128,2048]{2,1,0:T(8,128)} fusion(f32[9,128,2048]{2,1,0:T(8,128)S(1)} %fusion.17, f32[9,128,128]{2,1,0:T(8,128)} %bitcast.43, pred[128,128]{1,0:T(8,128)(4,1)S(1)} %iota_compare_fusion.2), kind=kOutput, calls=%fused_computation.9 | convolution fusion | flops 3624026112 | bytes 19480576 | tf_op jit(solution)/shard_map/kij,kjc->kic/dot_general | solution.py:33
  379.7 25.0 %convolution_subtract_fusion = f32[9,256,2048]{2,1,0:T(8,128)} fusion(f32[9,256,2048]{2,1,0:T(8,128)} %bitcast.35, f32[9,256,128]{2,1,0:T(8,128)S(1)} %bitcast.40, f32[9,128,2048]{2,1,0:T(8,128)} %fusion), kind=kOutput, calls=%fused_computation.3 | convolution fusion | flops 7252475904 | bytes 48365568 | tf_op jit(solution)/shard_map/kri,kic->krc/dot_general | solution.py:34
  404.7 29.7 %convolution_bitcast_fusion = f32[256,2048]{0,1:T(8,128)} fusion(f32[2048,256]{1,0:T(8,128)S(1)} %copy-done, f32[2304,2048]{1,0:T(8,128)} %bitcast.36), kind=kOutput, calls=%fused_computation.4 | convolution fusion | flops 12884901888 | bytes 20971520 | tf_op jit(solution)/shard_map/dot_general | solution.py:65
  434.5 11.8 %slice.26 = f32[2048,2048]{1,0:T(8,128)} slice(f32[2304,2048]{1,0:T(8,128)} %bitcast.37), slice={[128:2176], [0:2048]} | slice | bytes 33554432
  446.3 18.2 %copy.52 = f32[2048,2048]{0,1:T(8,128)} copy(f32[2048,2048]{1,0:T(8,128)} %slice.26) | data formatting | bytes 33554432
  464.5 35.2 %all-reduce.2.cloned.1.call-done = f32[256,2048]{0,1:T(8,128)} async-done(((f32[256,2048]{0,1:T(8,128)}), f32[256,2048]{0,1:T(8,128)}) %all-reduce.2.cloned.1.call-update) | async-done | bytes 2097168 | tf_op jit(solution)/shard_map/psum | solution.py:68
  499.7 3.5 fusion.6
  503.3 33.4 %bitcast_subtract_fusion = f32[2048,2048]{0,1:T(8,128)} fusion(f32[2048,2048]{0,1:T(8,128)} %copy.52, f32[256,2048]{1,0:T(8,128)S(1)} %fusion.6, f32[2048,256]{1,0:T(8,128)S(1)} %copy-done), kind=kOutput, calls=%fused_computation.1 | convolution fusion | flops 12889096192 | bytes 37748736 | tf_op jit(solution)/shard_map/dot_general | solution.py:72
  536.7 17.6 %copy.48 = f32[2048,2048]{1,0:T(8,128)} copy(f32[2048,2048]{0,1:T(8,128)} %bitcast_subtract_fusion) | data formatting | bytes 33554432 | tf_op jit(solution)/shard_map/sub | solution.py:72
  (39 shorter events, 4.5 us)
Async XLA Ops:
  6.5 398.2 %copy-start = (f32[2048,256]{1,0:T(8,128)S(1)}, f32[2048,256]{1,0:T(8,128)}, u32[]{:S(2)}) copy-start(f32[2048,256]{1,0:T(8,128)} %param.12) | copy-start | bytes 6291460
  6.5 8.7 %copy-start.6 = (f32[1024,32]{0,1:T(8,128)S(1)}, f32[1024,32]{0,1:T(8,128)}, u32[]{:S(2)}) copy-start(f32[1024,32]{0,1:T(8,128)} %param.10) | copy-start | bytes 393220
  6.5 190.8 %all-to-all-start = ((f32[4,2048,512]{2,1,0:T(8,128)}), f32[4,2048,512]{2,1,0:T(8,128)}, u32[]{:S(2)}, u32[]{:S(2)}) async-start(f32[4,2048,512]{2,1,0:T(8,128)} %bitcast.38), calls=%async_computation | async-start | bytes 33554432 | tf_op jit(solution)/shard_map/all_to_all | solution.py:61
  13.7 36.1 %all-gather.3.cloned.1.call-start = ((), (), s32[]{:S(2)}) async-start(), calls=%async_computation.1 | async-start | bytes 1310720 | tf_op jit(solution)/shard_map/all_gather | solution.py:88
  14.4 64.1 %all-gather.5.cloned.1.call-start = ((), (), s32[]{:S(2)}) async-start(), calls=%async_computation.2 | async-start | bytes 1310720 | tf_op jit(solution)/shard_map/all_gather | solution.py:89
  15.1 484.6 %all-reduce.2.cloned.1.call-start = ((), (), s32[]{:S(2)}) async-start(), calls=%async_computation.3 | async-start | bytes 4194304 | tf_op jit(solution)/shard_map/psum | solution.py:68
  238.8 14.5 %copy-start.4 = (f32[1024,128]{1,0:T(8,128)S(1)}, f32[1024,128]{1,0:T(8,128)}, u32[]{:S(2)}) copy-start(f32[1024,128]{1,0:T(8,128)} %copy.51) | copy-start | bytes 1572868
  253.3 9.6 %copy-start.3 = (f32[2048,128]{1,0:T(8,128)S(1)}, f32[2048,128]{1,0:T(8,128)}, u32[]{:S(2)}) copy-start(f32[2048,128]{1,0:T(8,128)} %copy.41) | copy-start | bytes 3145732
  285.4 6.7 %copy-start.7 = (f32[1024,32]{0,1:T(8,128)S(1)}, f32[1024,32]{0,1:T(8,128)}, u32[]{:S(2)}) copy-start(f32[1024,32]{0,1:T(8,128)} %param.11) | copy-start | bytes 393220
  288.5 29.8 %collective-permute-start = (f32[128,2176]{1,0:T(8,128)}, f32[128,2176]{1,0:T(8,128)}, u32[]{:S(2)}, u32[]{:S(2)}) collective-permute-start(f32[128,2176]{1,0:T(8,128)} %get-tuple-element.5), channel_id=1, source_target_pairs={{0,1},{1,2},{2,3},{3,16},{16,17},{17,18},{18,19},{4,5},{5,6},{6,7}... | collective-permute-start | bytes 3342344 | tf_op jit(solution)/shard_map/ppermute | solution.py:14
  290.8 27.5 %collective-permute-start.1 = (f32[128,2176]{1,0:T(8,128)}, f32[128,2176]{1,0:T(8,128)}, u32[]{:S(2)}, u32[]{:S(2)}) collective-permute-start(f32[128,2176]{1,0:T(8,128)} %get-tuple-element.6), channel_id=1, source_target_pairs={{1,0},{2,1},{3,2},{16,3},{17,16},{18,17},{19,18},{5,4},{6,5},{7,6}... | collective-permute-start | bytes 3342344 | tf_op jit(solution)/shard_map/ppermute | solution.py:15
  313.2 3.1 collective-permute-start.2
  318.3 34.6 %slice-start = ((s8[16777216]{0:T(1024)(128)(4,1)}), s8[4194304]{0:T(1024)(128)(4,1)S(1)}, s32[]{:S(2)}) async-start(s8[16777216]{0:T(1024)(128)(4,1)} %bitcast.31), calls=%async_computation.4 | async-start | bytes 8388608
  318.3 34.6 %slice-start.1 = ((s8[16777216]{0:T(1024)(128)(4,1)}), s8[4194304]{0:T(1024)(128)(4,1)S(1)}, s32[]{:S(2)}) async-start(s8[16777216]{0:T(1024)(128)(4,1)} %bitcast.31), calls=%async_computation.5 | async-start | bytes 8388608
  318.3 34.6 %slice-start.2 = ((s8[16777216]{0:T(1024)(128)(4,1)}), s8[4194304]{0:T(1024)(128)(4,1)S(1)}, s32[]{:S(2)}) async-start(s8[16777216]{0:T(1024)(128)(4,1)} %bitcast.31), calls=%async_computation.6 | async-start | bytes 8388608
  337.4 15.5 %slice-start.3 = ((s8[16777216]{0:T(1024)(128)(4,1)}), s8[4194304]{0:T(1024)(128)(4,1)S(1)}, s32[]{:S(2)}) async-start(s8[16777216]{0:T(1024)(128)(4,1)} %bitcast.31), calls=%async_computation.7 | async-start | bytes 8388608
  353.9 14.0 %copy-start.1 = (f32[2304,128]{1,0:T(8,128)}, f32[2304,128]{1,0:T(8,128)S(1)}, u32[]{:S(2)}) copy-start(f32[2304,128]{1,0:T(8,128)S(1)} %pad_maximum_fusion.1) | copy-start | bytes 3538948
  367.9 11.9 %copy-start.2 = (f32[2304,128]{1,0:T(8,128)S(1)}, f32[2304,128]{1,0:T(8,128)}, u32[]{:S(2)}) copy-start(f32[2304,128]{1,0:T(8,128)} %copy-done.1) | copy-start | bytes 3538948
  446.3 53.5 %copy-start.5 = (f32[256,256]{1,0:T(8,128)S(1)}, f32[256,256]{1,0:T(8,128)}, u32[]{:S(2)}) copy-start(f32[256,256]{1,0:T(8,128)} %param.13) | copy-start | bytes 786436
Sparse Core Ops, SparseCore 0:
  16.0 33.7 all-gather.2
  51.4 27.1 all-gather.4
  434.6 65.1 all-reduce.1
where the time goes:
time: 572 us; the launch traced here: 561 us
  waiting for transfers between devices  195 us (34%)
  matrix products  164 us (29%)
  local copies, waits for them, and re-layouts  113 us (20%)
  blocking collectives  38.4 us (7%)
  other arithmetic  25.2 us (4%)
  between operations  13.7 us (2%)
  starting transfers between devices  12.1 us (2%)
    all_to_all x1, waiting for transfers between devices, to_tiles(): lax.all_to_all(data, 'layer', split_axis=0, concat_axis=1, tiled=True)  117 us
    dot_general x2, matrix products, apply_windows(): jnp.einsum('kri,kic->krc', vec_blocks, scaled, precision=lax.Precision.HI...  47.4 us
    psum x1, waiting for transfers between devices, panel_tile(): projection = lax.psum(partial_value, ('row', 'layer'))  35.2 us
    dot_general x1, matrix products, panel_tile(): jnp.dot(panel_vectors, weights, precision=lax.Precision.HIGHEST, preferre...  33.4 us
    unnamed x26, local copies, waits for them, and re-layouts  30.1 us
    dot_general x1, matrix products, panel_tile(): jnp.dot(panel_vectors.T, data, precision=lax.Precision.HIGHEST, preferred...  29.7 us
    dot_general x2, matrix products, apply_windows(): jnp.einsum('kri,krc->kic', vec_blocks, blocks, precision=lax.Precision.HI...  28.5 us
    all_gather x1, waiting for transfers between devices, on_device(): lax.all_gather(second_vectors, 'col', axis=1, tiled=True)  26.1 us
  transfers between devices with their start and end apart: 7, of which 5 were waited for; matrix products, arithmetic and copies ran while one was open for 7% of the time, Pallas kernels for 0%

commit v1 on v0

--- a/solution.py
+++ b/solution.py
@@ -2,6 +2,13 @@
 import jax.numpy as jnp
 from jax import lax
 from jax.sharding import PartitionSpec as P
+
+
+def swap_blocks(x, mesh_axis, split, join):
+    n_dev = lax.axis_size(mesh_axis)
+    blocks = jnp.stack(jnp.split(x, n_dev, axis=split), axis=0)
+    blocks = lax.all_to_all(blocks, mesh_axis, split_axis=0, concat_axis=0)
+    return jnp.concatenate(blocks, axis=join)
 
 
 def with_halo(array, sides, width):
@@ -58,7 +65,7 @@
 
 
 def to_tiles(data):
-    return lax.all_to_all(data, "layer", split_axis=0, concat_axis=1, tiled=True)
+    return swap_blocks(data, "layer", 0, 1)
 
 
 def panel_tile(data, panel_vectors, upper):

time: 572 us -> 600 us (1.049)
  matrix products: 164 us -> 179 us
  other arithmetic: 25.2 us -> 31.6 us
  local copies, waits for them, and re-layouts: 113 us -> 119 us
    another operation x0 -> x3, local copies, waits for them, and re-layouts: none -> 48.5 us  [the longest x2 41.4 us: apply_windows(): blocks = data.reshape(count, 256, width)]
    all_to_all x1 -> x0, local copies, waits for them, and re-layouts: 20.9 us -> none  [to_tiles(): lax.all_to_all(data, 'layer', split_axis=0, concat_axis=1, tiled=True)]
    reshape x1 -> x0, local copies, waits for them, and re-layouts: 20.5 us -> none  [apply_windows(): blocks = data.reshape(count, 256, width)]
    dot_general x2, matrix products: 28.5 us -> 43.7 us  [apply_windows(): jnp.einsum('kri,krc->kic', vec_blocks, blocks, precision=lax.Precision.HI...]
    another operation x0 -> x1, other arithmetic: none -> 6.38 us  [swap_blocks(): blocks = jnp.stack(jnp.split(x, n_dev, axis=split), axis=0)]
where the time goes in v1:
time: 600 us; the launch traced here: 590 us
  waiting for transfers between devices  195 us (32%)
  matrix products  179 us (30%)
  local copies, waits for them, and re-layouts  119 us (20%)
  blocking collectives  38.4 us (6%)
  other arithmetic  31.6 us (5%)
  between operations  13.5 us (2%)
  starting transfers between devices  12.1 us (2%)
    all_to_all x1, waiting for transfers between devices, swap_blocks(): blocks = lax.all_to_all(blocks, mesh_axis, split_axis=0, concat_axis=0)  117 us
    dot_general x2, matrix products, apply_windows(): jnp.einsum('kri,kic->krc', vec_blocks, scaled, precision=lax.Precision.HI...  47.4 us
    dot_general x2, matrix products, apply_windows(): jnp.einsum('kri,krc->kic', vec_blocks, blocks, precision=lax.Precision.HI...  43.7 us
    another operation x2, local copies, waits for them, and re-layouts, apply_windows(): blocks = data.reshape(count, 256, width)  41.4 us
    psum x1, waiting for transfers between devices, panel_tile(): projection = lax.psum(partial_value, ('row', 'layer'))  35.4 us
    dot_general x1, matrix products, panel_tile(): jnp.dot(panel_vectors, weights, precision=lax.Precision.HIGHEST, preferre...  33.3 us
    unnamed x26, local copies, waits for them, and re-layouts  29.9 us
    dot_general x1, matrix products, panel_tile(): jnp.dot(panel_vectors.T, data, precision=lax.Precision.HIGHEST, preferred...  29.7 us
  transfers between devices with their start and end apart: 7, of which 5 were waited for; matrix products, arithmetic and copies ran while one was open for 7% of the time, Pallas kernels for 0%

profile of v1, /device:TPU:0, one launch (start us, length us, event | category | flops | bytes accessed | tf_op | source)
XLA Modules:
  0.0 589.7 jit_solution(11896225304437344640)
XLA Ops:
  6.5 7.0 %slice_bitcast_fusion.3 = (f32[1,2048,512]{2,1,0:T(8,128)S(1)}, f32[1,2048,512]{2,1,0:T(8,128)S(1)}, f32[1,2048,512]{2,1,0:T(8,128)S(1)}, f32[1,2048,512]{2,1,0:T(8,128)S(1)}) fusion(f32[8192,512]{1,0:T(8,128)} %param.7), kind=kLoop, calls=%fused_computation.8 | loop fusion | bytes 33554432 | tf_op jit(solution)/shard_map/stack | solution.py:9
  13.6 6.4 %pad_maximum_fusion.1 = f32[4,2048,512]{2,1,0:T(8,128)} fusion(f32[1,2048,512]{2,1,0:T(8,128)S(1)} %get-tuple-element.9, f32[1,2048,512]{2,1,0:T(8,128)S(1)} %get-tuple-element.10, f32[1,2048,512]{2,1,0:T(8,128)S(1)} %get-tuple-element.8, f32[1,2048,512]{2,1,0:T(8,128)S(1)} %get-tuple-element.7), kind=kLoop, calls=%fused_computation.1 | loop fusion | flops 12582912 | bytes 33554432 | tf_op jit(solution)/shard_map/stack | solution.py:9
  20.0 7.1 %all-to-all-start = ((f32[4,2048,512]{2,1,0:T(8,128)}), f32[4,2048,512]{2,1,0:T(8,128)}, u32[]{:S(2)}, u32[]{:S(2)}) async-start(f32[4,2048,512]{2,1,0:T(8,128)} %pad_maximum_fusion.1), calls=%async_computation | async-start | bytes 33554432 | tf_op jit(solution)/shard_map/all_to_all | solution.py:10
  28.6 20.1 %all_gather.12 = f32[1024,128]{0,1:T(8,128)S(1)} all-gather(f32[1024,32]{0,1:T(8,128)S(1)} %copy-done.6), channel_id=1, replica_groups=mesh['row'=2,'col'=4,'layer'=4] {'col'}, dimensions={1}, use_global_device_ids=true | all-gather | bytes 655360 | tf_op jit(solution)/shard_map/all_gather | solution.py:97
  49.9 13.4 %all-gather.3.cloned.1.call-done = f32[2048,128]{0,1:T(8,128)} async-done(((f32[2048,32]{0,1:T(8,128)}), f32[2048,128]{0,1:T(8,128)}) %all-gather.3.cloned.1.call-update) | async-done | bytes 1048592 | tf_op jit(solution)/shard_map/all_gather | solution.py:95
  63.2 2.6 copy.42
  65.9 26.1 %all-gather.5.cloned.1.call-done = f32[2048,128]{0,1:T(8,128)} async-done(((f32[2048,32]{0,1:T(8,128)}), f32[2048,128]{0,1:T(8,128)}) %all-gather.5.cloned.1.call-update) | async-done | bytes 1048592 | tf_op jit(solution)/shard_map/all_gather | solution.py:96
  92.0 1.5 copy.45
  93.5 117.2 %all-to-all-done = f32[4,2048,512]{2,1,0:T(8,128)} async-done(((f32[4,2048,512]{2,1,0:T(8,128)}), f32[4,2048,512]{2,1,0:T(8,128)}, u32[]{:S(2)}, u32[]{:S(2)}) %all-to-all-start) | async-done | bytes 16777248 | tf_op jit(solution)/shard_map/all_to_all | solution.py:10
  210.8 20.9 %copy.54 = f32[2048,4,512]{2,1,0:T(4,128)} copy(f32[2048,4,512]{2,0,1:T(8,128)} %bitcast.4) | data formatting | bytes 33554432 | tf_op jit(solution)/shard_map/reshape;reshape | solution.py:36
  231.7 20.5 %reshape.32 = f32[8,256,2048]{2,1,0:T(8,128)} reshape(f32[2048,4,512]{2,1,0:T(4,128)} %copy.54) | data formatting | bytes 33554432 | tf_op jit(solution)/shard_map/reshape;reshape | solution.py:36
  252.2 29.7 %fusion.16 = f32[8,2048,128]{2,1,0:T(8,128)S(1)} fusion(f32[8,256,2048]{2,1,0:T(8,128)} %reshape.32, f32[8,256,128]{2,1,0:T(8,128)} %bitcast.47), kind=kOutput, calls=%fused_computation.34 | convolution fusion | flops 6442450944 | bytes 26214400 | tf_op jit(solution)/shard_map/kri,krc->kic/dot_general | solution.py:39
  282.0 9.8 %fusion.2 = f32[8,128,2048]{2,1,0:T(8,128)} fusion(f32[8,2048,128]{2,1,0:T(8,128)S(1)} %fusion.16, f32[8,128,128]{2,1,0:T(8,128)S(1)} %bitcast.50, pred[128,128]{1,0:T(8,128)(4,1)S(1)} %iota_compare_fusion.2), kind=kOutput, calls=%fused_computation.16 | convolution fusion | flops 3221356544 | bytes 17317888 | tf_op jit(solution)/shard_map/kij,kjc->kic/dot_general | solution.py:40
  291.7 22.3 %bitcast_subtract_fusion.1 = f32[8,256,2048]{2,1,0:T(8,128)} fusion(f32[8,256,2048]{2,1,0:T(8,128)} %reshape.32, f32[8,128,2048]{2,1,0:T(8,128)} %fusion.2, f32[8,256,128]{2,1,0:T(8,128)S(1)} %bitcast.48), kind=kOutput, calls=%fused_computation.3 | convolution fusion | flops 6446645248 | bytes 42991616 | tf_op jit(solution)/shard_map/kri,kic->krc/dot_general | solution.py:41
  314.0 3.1 pad_maximum_fusion.4
  317.2 2.3 collective-permute-start
  320.7 18.3 %all_gather.15 = f32[1024,128]{0,1:T(8,128)} all-gather(f32[1024,32]{0,1:T(8,128)S(1)} %copy-done.7), channel_id=1, replica_groups=mesh['row'=2,'col'=4,'layer'=4] {'col'}, dimensions={1}, use_global_device_ids=true | all-gather | bytes 655360 | tf_op jit(solution)/shard_map/all_gather | solution.py:98
  339.0 2.0 copy.47
  343.2 1.8 collective-permute-done.2
  345.1 1.9 pad_maximum_fusion.5
  347.0 19.1 %pad_maximum_fusion = f32[2304,2176]{1,0:T(8,128)} fusion(f32[128,2176]{1,0:T(8,128)} %collective-permute-done.1, f32[2048,128]{1,0:T(8,128)S(1)} %copy.45, f32[2048,2048]{1,0:T(8,128)} %bitcast.37, f32[128,2176]{1,0:T(8,128)} %collective-permute-done), kind=kLoop, calls=%fused_computation | loop fusion | flops 15040512 | bytes 40108032 | tf_op jit(solution)/shard_map/concatenate | solution.py:23
  366.1 15.5 %slice.24 = f32[2304,2048]{1,0:T(8,128)} slice(f32[2304,2176]{1,0:T(8,128)} %pad_maximum_fusion), slice={[0:2304], [0:2048]} | slice | bytes 37748736 | tf_op jit(solution)/shard_map/slice | solution.py:52
  382.6 14.0 %fusion.17 = f32[9,128,2048]{2,1,0:T(8,128)S(1)} fusion(f32[9,256,128]{2,1,0:T(8,128)S(1)} %bitcast.45, f32[9,256,2048]{2,1,0:T(8,128)} %bitcast.41), kind=kOutput, calls=%fused_computation.35 | convolution fusion | flops 7247757312 | bytes 29491200 | tf_op jit(solution)/shard_map/kri,krc->kic/dot_general | solution.py:39
  396.6 11.8 %fusion = f32[9,128,2048]{2,1,0:T(8,128)} fusion(f32[9,128,2048]{2,1,0:T(8,128)S(1)} %fusion.17, f32[9,128,128]{2,1,0:T(8,128)} %bitcast.49, pred[128,128]{1,0:T(8,128)(4,1)S(1)} %iota_compare_fusion.2), kind=kOutput, calls=%fused_computation.14 | convolution fusion | flops 3624026112 | bytes 19480576 | tf_op jit(solution)/shard_map/kij,kjc->kic/dot_general | solution.py:40
  408.4 25.1 %convolution_subtract_fusion = f32[9,256,2048]{2,1,0:T(8,128)} fusion(f32[9,256,2048]{2,1,0:T(8,128)} %bitcast.42, f32[9,256,128]{2,1,0:T(8,128)S(1)} %bitcast.46, f32[9,128,2048]{2,1,0:T(8,128)} %fusion), kind=kOutput, calls=%fused_computation.4 | convolution fusion | flops 7252475904 | bytes 48365568 | tf_op jit(solution)/shard_map/kri,kic->krc/dot_general | solution.py:41
  433.6 29.7 %convolution_bitcast_fusion = f32[256,2048]{0,1:T(8,128)} fusion(f32[2048,256]{1,0:T(8,128)S(1)} %copy-done, f32[2304,2048]{1,0:T(8,128)} %bitcast.43), kind=kOutput, calls=%fused_computation.9 | convolution fusion | flops 12884901888 | bytes 20971520 | tf_op jit(solution)/shard_map/dot_general | solution.py:72
  463.3 11.8 %slice.26 = f32[2048,2048]{1,0:T(8,128)} slice(f32[2304,2048]{1,0:T(8,128)} %bitcast.44), slice={[128:2176], [0:2048]} | slice | bytes 33554432
  475.1 18.0 %copy.53 = f32[2048,2048]{0,1:T(8,128)} copy(f32[2048,2048]{1,0:T(8,128)} %slice.26) | data formatting | bytes 33554432
  493.1 35.4 %all-reduce.2.cloned.1.call-done = f32[256,2048]{0,1:T(8,128)} async-done(((f32[256,2048]{0,1:T(8,128)}), f32[256,2048]{0,1:T(8,128)}) %all-reduce.2.cloned.1.call-update) | async-done | bytes 2097168 | tf_op jit(solution)/shard_map/psum | solution.py:75
  528.6 3.5 fusion.6
  532.1 33.3 %bitcast_subtract_fusion = f32[2048,2048]{0,1:T(8,128)} fusion(f32[2048,2048]{0,1:T(8,128)} %copy.53, f32[256,2048]{1,0:T(8,128)S(1)} %fusion.6, f32[2048,256]{1,0:T(8,128)S(1)} %copy-done), kind=kOutput, calls=%fused_computation.2 | convolution fusion | flops 12889096192 | bytes 37748736 | tf_op jit(solution)/shard_map/dot_general | solution.py:79
  565.3 17.6 %copy.50 = f32[2048,2048]{1,0:T(8,128)} copy(f32[2048,2048]{0,1:T(8,128)} %bitcast_subtract_fusion) | data formatting | bytes 33554432 | tf_op jit(solution)/shard_map/sub | solution.py:79
  (41 shorter events, 7.0 us)
Async XLA Ops:
  6.5 427.0 %copy-start = (f32[2048,256]{1,0:T(8,128)S(1)}, f32[2048,256]{1,0:T(8,128)}, u32[]{:S(2)}) copy-start(f32[2048,256]{1,0:T(8,128)} %param.12) | copy-start | bytes 6291460
  20.0 8.7 %copy-start.6 = (f32[1024,32]{0,1:T(8,128)S(1)}, f32[1024,32]{0,1:T(8,128)}, u32[]{:S(2)}) copy-start(f32[1024,32]{0,1:T(8,128)} %param.10) | copy-start | bytes 393220
  20.0 190.8 %all-to-all-start = ((f32[4,2048,512]{2,1,0:T(8,128)}), f32[4,2048,512]{2,1,0:T(8,128)}, u32[]{:S(2)}, u32[]{:S(2)}) async-start(f32[4,2048,512]{2,1,0:T(8,128)} %pad_maximum_fusion.1), calls=%async_computation | async-start | bytes 33554432 | tf_op jit(solution)/shard_map/all_to_all | solution.py:10
  27.1 36.1 %all-gather.3.cloned.1.call-start = ((), (), s32[]{:S(2)}) async-start(), calls=%async_computation.1 | async-start | bytes 1310720 | tf_op jit(solution)/shard_map/all_gather | solution.py:95
  27.8 64.1 %all-gather.5.cloned.1.call-start = ((), (), s32[]{:S(2)}) async-start(), calls=%async_computation.2 | async-start | bytes 1310720 | tf_op jit(solution)/shard_map/all_gather | solution.py:96
  28.6 500.0 %all-reduce.2.cloned.1.call-start = ((), (), s32[]{:S(2)}) async-start(), calls=%async_computation.3 | async-start | bytes 4194304 | tf_op jit(solution)/shard_map/psum | solution.py:75
  252.2 29.8 %copy-start.4 = (f32[1024,128]{1,0:T(8,128)S(1)}, f32[1024,128]{1,0:T(8,128)}, u32[]{:S(2)}) copy-start(f32[1024,128]{1,0:T(8,128)} %copy.52) | copy-start | bytes 1572868
  281.9 9.8 %copy-start.3 = (f32[2048,128]{1,0:T(8,128)S(1)}, f32[2048,128]{1,0:T(8,128)}, u32[]{:S(2)}) copy-start(f32[2048,128]{1,0:T(8,128)} %copy.42) | copy-start | bytes 3145732
  314.0 6.7 %copy-start.7 = (f32[1024,32]{0,1:T(8,128)S(1)}, f32[1024,32]{0,1:T(8,128)}, u32[]{:S(2)}) copy-start(f32[1024,32]{0,1:T(8,128)} %param.11) | copy-start | bytes 393220
  317.2 29.8 %collective-permute-start = (f32[128,2176]{1,0:T(8,128)}, f32[128,2176]{1,0:T(8,128)}, u32[]{:S(2)}, u32[]{:S(2)}) collective-permute-start(f32[128,2176]{1,0:T(8,128)} %get-tuple-element.5), channel_id=1, source_target_pairs={{0,1},{1,2},{2,3},{3,16},{16,17},{17,18},{18,19},{4,5},{5,6},{6,7}... | collective-permute-start | bytes 3342344 | tf_op jit(solution)/shard_map/ppermute | solution.py:21
  319.4 27.6 %collective-permute-start.1 = (f32[128,2176]{1,0:T(8,128)}, f32[128,2176]{1,0:T(8,128)}, u32[]{:S(2)}, u32[]{:S(2)}) collective-permute-start(f32[128,2176]{1,0:T(8,128)} %get-tuple-element.6), channel_id=1, source_target_pairs={{1,0},{2,1},{3,2},{16,3},{17,16},{18,17},{19,18},{5,4},{6,5},{7,6}... | collective-permute-start | bytes 3342344 | tf_op jit(solution)/shard_map/ppermute | solution.py:22
  341.9 3.1 collective-permute-start.2
  347.0 34.6 %slice-start = ((s8[16777216]{0:T(1024)(128)(4,1)}), s8[4194304]{0:T(1024)(128)(4,1)S(1)}, s32[]{:S(2)}) async-start(s8[16777216]{0:T(1024)(128)(4,1)} %bitcast.38), calls=%async_computation.4 | async-start | bytes 8388608
  347.0 34.6 %slice-start.1 = ((s8[16777216]{0:T(1024)(128)(4,1)}), s8[4194304]{0:T(1024)(128)(4,1)S(1)}, s32[]{:S(2)}) async-start(s8[16777216]{0:T(1024)(128)(4,1)} %bitcast.38), calls=%async_computation.5 | async-start | bytes 8388608
  347.0 34.6 %slice-start.2 = ((s8[16777216]{0:T(1024)(128)(4,1)}), s8[4194304]{0:T(1024)(128)(4,1)S(1)}, s32[]{:S(2)}) async-start(s8[16777216]{0:T(1024)(128)(4,1)} %bitcast.38), calls=%async_computation.6 | async-start | bytes 8388608
  366.1 15.5 %slice-start.3 = ((s8[16777216]{0:T(1024)(128)(4,1)}), s8[4194304]{0:T(1024)(128)(4,1)S(1)}, s32[]{:S(2)}) async-start(s8[16777216]{0:T(1024)(128)(4,1)} %bitcast.38), calls=%async_computation.7 | async-start | bytes 8388608
  382.6 14.0 %copy-start.1 = (f32[2304,128]{1,0:T(8,128)}, f32[2304,128]{1,0:T(8,128)S(1)}, u32[]{:S(2)}) copy-start(f32[2304,128]{1,0:T(8,128)S(1)} %pad_maximum_fusion.2) | copy-start | bytes 3538948
  396.6 11.9 %copy-start.2 = (f32[2304,128]{1,0:T(8,128)S(1)}, f32[2304,128]{1,0:T(8,128)}, u32[]{:S(2)}) copy-start(f32[2304,128]{1,0:T(8,128)} %copy-done.1) | copy-start | bytes 3538948
  475.1 53.4 %copy-start.5 = (f32[256,256]{1,0:T(8,128)S(1)}, f32[256,256]{1,0:T(8,128)}, u32[]{:S(2)}) copy-start(f32[256,256]{1,0:T(8,128)} %param.13) | copy-start | bytes 786436
Sparse Core Ops, SparseCore 0:
  29.5 33.7 all-gather.2
  64.8 27.1 all-gather.4
  463.4 65.0 all-reduce.1
